TPU v7x, 512 devices: a whole 4x4x16 slice. The times are simulated.
512 devices in a mesh: dp: 32 (over z, core), shard: 16 (over y, x).
Axes of the slice: x: 4, y: 4, z: 16, core: 2. Of those that a mesh axis runs over, the one named last changes fastest.
Arguments:
- points: bfloat16 [131072, 1024], P(('dp', 'shard'))
- first_center: bfloat16 [1024], replicated, may hold values from -0.1875 to 0.1875
- counts: int32 [3, 32, 16], P(None, 'dp', 'shard'), may hold values from 0 to 4, as said below
- cand_index: int32 [3, 32, 16, 4], P(None, 'dp', 'shard'), may hold values from 0 to 255, as said below
Outputs:
- min_dist: float32 [131072], P(('dp', 'shard'))
- weights: float32 [131072], P(('dp', 'shard'))
- potentials: float32 [4], replicated
Inputs may be any that keep to these rules, and one draw needn't show every extreme that they name: In each round the counts of the 16 devices of one dp index sum to 16, so a round has 512 candidates; in each round and dp index some device has exactly 4. `cand_index`: each device's list in a round holds distinct local row numbers; only its first counts entries are candidates.
All inputs are finite; a program needn't handle non-finite values.
Results may differ from a plain program's by a relative error of at most 0.0003.
Values may be sent and summed in bfloat16 or wider, within the bound.
No kernel may reach another device: no remote copies, remote signals or barrier semaphores. Data moves between devices by JAX's collectives and lax.ppermute only.
A program may use at most 64 MiB of HBM per device.

v0:
```python
import jax
import jax.numpy as jnp
from jax import lax
from jax.sharding import PartitionSpec as P


def pair_dist(rows, rows_norm, cands):
    prod = jnp.dot(rows, cands.T, preferred_element_type=jnp.float32)
    cand_norm = jnp.sum(jnp.square(cands.astype(jnp.float32)), axis=1)
    return jnp.maximum(rows_norm[:, None] + cand_norm[None, :] - 2.0 * prod, 0.0)


def body(points, first_center, counts, cand_index):
    rows_norm = jnp.sum(jnp.square(points.astype(jnp.float32)), axis=1)
    running = jnp.min(pair_dist(points, rows_norm, first_center[None, :]), axis=1)
    rounds = counts.shape[0]
    cap = cand_index.shape[3]
    every_count = lax.all_gather(counts.reshape(rounds, 1), ("dp", "shard"), axis=1, tiled=True)
    devices_all = every_count.shape[1]

    def global_sum(value):
        return lax.psum(value, ("dp", "shard"))

    partials = [jnp.sum(running)]
    totals = [global_sum(partials[0])]
    for step in range(rounds):
        local_rows = jnp.take(points, cand_index[step, 0, 0], axis=0)
        slot_limit = jnp.repeat(every_count[step], cap)
        slot_pos = jnp.tile(jnp.arange(cap, dtype=jnp.int32), devices_all)
        live = slot_pos < slot_limit

        def fold_flat(carry, piece, start, live=live):
            dist = pair_dist(points, rows_norm, piece)
            dist = jnp.where(live[None, :], dist, jnp.inf)
            return jnp.minimum(carry, jnp.min(dist, axis=1))

        running = fold_flat(
            running, lax.all_gather(local_rows, ("dp", "shard"), axis=0, tiled=True), jnp.int32(0)
        )
        partials.append(jnp.sum(running))
        totals.append(global_sum(partials[-1]))
    potentials = jnp.stack(totals)
    rows_total = points.shape[0] * lax.axis_size("dp") * lax.axis_size("shard")
    weights = running * (rows_total / potentials[-1])
    return (running, weights, potentials)


def solution(mesh):
    placed = (P(("dp", "shard"), None), P(), P(None, "dp", "shard"), P(None, "dp", "shard", None))
    return jax.shard_map(
        body,
        mesh=mesh,
        in_specs=placed,
        out_specs=(P(("dp", "shard")), P(("dp", "shard")), P()),
        check_vma=False,
    )
```

profile of v0, /device:TPU:1, one launch (start us, length us, event | category | flops | bytes accessed | tf_op | source)
XLA Modules:
  0.0 746.0 jit_solution(109558366901745386)
XLA Ops:
  7.2 0.0 copy-start.4
  7.2 0.0 all-gather.12.cloned.1.call-start
  7.2 0.7 compare_and_fusion.2
  8.0 1.7 gather_fusion.2
  9.7 0.7 select_bitcast_fusion
  10.3 0.0 all-gather.12.cloned.1.call-update
  10.4 0.0 all-gather.10.cloned.1.call-start
  10.4 1.7 gather_fusion.1
  12.1 0.7 select_bitcast_fusion.1
  12.8 0.0 all-gather.10.cloned.1.call-update
  12.8 0.0 all-gather.8.cloned.1.call-start
  12.9 1.7 gather_fusion
  14.6 0.7 select_bitcast_fusion.2
  15.2 0.0 all-gather.8.cloned.1.call-update
  15.2 189.0 %all-gather = s32[3,512,1]{0,2,1:T(1,128)S(1)} all-gather(s32[3,1,1]{0,2,1:T(1,128)} %param.8), channel_id=2, replica_groups=mesh['dp'=32,'shard'=16] {'dp','shard'}, dimensions={1}, use_global_device_ids=true | all-gather | bytes 6156 | tf_op jit(solution)/shard_map/all_gather | solution.py:18
  204.2 28.8 %slice_reduce_fusion.2 = (s32[512]{0:T(512)S(1)}, s32[512]{0:T(512)S(1)}, s32[512]{0:T(512)S(1)}) fusion(s32[3,512,1]{0,2,1:T(1,128)S(1)} %all-gather), kind=kLoop, calls=%fused_computation.27 | loop fusion | bytes 12288 | tf_op jit(solution)/shard_map/slice | solution.py:28
  233.0 0.1 iota_compare_fusion
  233.1 0.2 lt.38
  233.3 0.1 iota_compare_fusion.1
  233.5 0.2 lt.36
  233.7 0.1 iota_compare_fusion.2
  233.8 0.2 lt.34
  234.0 0.7 reshape.114
  234.7 1.3 multiply_reduce_fusion.4
  236.0 0.0 copy-done.4
  236.0 0.2 multiply_reduce_fusion.3
  236.2 0.2 fusion.16
  236.4 0.0 all-gather.12.cloned.1.call-done
  236.4 6.9 reshape.107
  243.4 172.3 %all-gather.10.cloned.1.call-done = bf16[512,4,1024]{2,1,0:T(4,128)(2,1)} async-done(((bf16[1,4,1024]{2,1,0:T(4,128)(2,1)}), bf16[512,4,1024]{2,1,0:T(4,128)(2,1)}) %all-gather.10.cloned.1.call-update) | async-done | bytes 4194320 | tf_op jit(solution)/shard_map/all_gather | solution.py:38
  415.6 6.9 reshape.105
  422.5 0.0 copy-start.1
  422.5 3.2 multiply_reduce_fusion
  425.8 0.2 copy-done.1
  426.0 0.9 multiply_reduce_fusion.1
  426.9 187.3 %all-gather.8.cloned.1.call-done = bf16[512,4,1024]{2,1,0:T(4,128)(2,1)} async-done(((bf16[1,4,1024]{2,1,0:T(4,128)(2,1)}), bf16[512,4,1024]{2,1,0:T(4,128)(2,1)}) %all-gather.8.cloned.1.call-update) | async-done | bytes 4194320 | tf_op jit(solution)/shard_map/all_gather | solution.py:38
  614.1 6.9 reshape.103
  621.0 0.0 copy-start
  621.1 3.2 multiply_reduce_fusion.2
  624.3 0.2 copy-done
  624.5 0.0 copy-start.2
  624.5 1.6 fusion.12
  626.1 0.6 copy-done.2
  626.7 0.0 copy-start.3
  626.7 1.6 fusion.13
  628.3 0.6 copy-done.3
  628.9 1.6 fusion.14
  630.5 1.3 minimum_reduce_fusion.1
  631.8 0.6 fusion.15
  632.4 0.0 copy-start.5
  632.4 102.7 %all-reduce = (f32[]{:T(128)}, f32[1]{0:T(128)}, f32[1]{0:T(128)}, f32[1]{0:T(128)}) all-reduce(f32[]{:T(128)} %get-tuple-element.15, f32[1]{0:T(128)} %bitcast.12, f32[1]{0:T(128)} %bitcast.11, f32[1]{0:T(128)} %bitcast.10), channel_id=1, replica_groups=mesh['dp'=32,'shard'=16] {'dp','shard'}, use_global_device_ids=true, to_apply=%region_9.11 | all-reduce | flops 4 | bytes 32 | tf_op jit(solution)/shard_map/psum | solution.py:22
  735.8 0.6 broadcast_multiply_fusion
  736.4 3.1 pad_maximum_fusion
  739.5 0.0 copy-done.5
  (3 shorter events, 0.0 us)
Async XLA Ops:
  7.2 228.8 %copy-start.4 = (bf16[256,1024]{1,0:T(8,128)(2,1)S(1)}, bf16[256,1024]{1,0:T(8,128)(2,1)}, u32[]{:S(2)}) copy-start(bf16[256,1024]{1,0:T(8,128)(2,1)} %param.6) | copy-start | bytes 1572868
  7.2 229.2 %all-gather.12.cloned.1.call-start = ((), (), s32[]{:S(2)}) async-start(), calls=%async_computation.2 | async-start | bytes 4202496 | tf_op jit(solution)/shard_map/all_gather | solution.py:38
  10.4 405.3 %all-gather.10.cloned.1.call-start = ((), (), s32[]{:S(2)}) async-start(), calls=%async_computation.1 | async-start | bytes 4202496 | tf_op jit(solution)/shard_map/all_gather | solution.py:38
  12.8 601.3 %all-gather.8.cloned.1.call-start = ((), (), s32[]{:S(2)}) async-start(), calls=%async_computation | async-start | bytes 4202496 | tf_op jit(solution)/shard_map/all_gather | solution.py:38
  422.5 3.4 copy-start.1
  621.0 3.4 copy-start
  624.5 2.2 copy-start.2
  626.7 2.2 copy-start.3
  632.4 107.1 %copy-start.5 = (f32[256]{0:T(256)}, f32[256]{0:T(256)S(1)}, u32[]{:S(2)}) copy-start(f32[256]{0:T(256)S(1)} %get-tuple-element.16) | copy-start | bytes 3076
Sparse Core Ops, SparseCore 0:
  12.4 203.7 all-gather.11
  220.6 194.9 all-gather.9
  420.1 194.0 all-gather.7
where the time goes:
time: 747 us; the launch traced here: 746 us
  waiting for transfers between devices  360 us (48%)
  blocking collectives  292 us (39%)
  local copies, waits for them, and re-layouts  57.6 us (8%)
  other arithmetic  17.6 us (2%)
  between operations  14.5 us (2%)
    all_gather x3, waiting for transfers between devices, body(): lax.all_gather(local_rows, ('dp', 'shard'), axis=0, tiled=True)  360 us
    all_gather x1, blocking collectives, body(): lax.all_gather(counts.reshape(rounds, 1), ('dp', 'shard'), axis=1, tiled=...  189 us
    psum x1, blocking collectives, global_sum(): return lax.psum(value, ('dp', 'shard'))  103 us
    slice x1, local copies, waits for them, and re-layouts, body(): slot_limit = jnp.repeat(every_count[step], cap)  28.8 us
    unnamed x16, local copies, waits for them, and re-layouts  23.1 us
  transfers between devices with their start and end apart: 3, of which 2 were waited for; matrix products, arithmetic and copies ran while one was open for 7% of the time, Pallas kernels for 0%

commit v1 on v0

v1 whole, which is shorter than its diff:
```python
import jax
import jax.numpy as jnp
from jax import lax
from jax.experimental import pallas as pl
from jax.experimental.pallas import tpu as pltpu
from jax.sharding import Mesh
from jax.sharding import PartitionSpec as P

D = 1024
ROWS_DEV = 256
ROUNDS = 3
CAP = 4
ROWS = 131072
NZ, NC, NY, NX = 16, 2, 4, 4
PLANE = NY * NX
BLK = 16
CNT_ROW = ROUNDS * CAP
KEEP = ROUNDS * NZ
HALF = KEEP * PLANE

VMEM = pltpu.VMEM
SMEM = pltpu.SMEM
F32 = jnp.float32
BF16 = jnp.bfloat16


def iota(shape, dim):
    return lax.broadcasted_iota(jnp.int32, shape, dim)


def one_hot(cond):
    return jnp.where(cond, 1.0, 0.0).astype(BF16)


def dot_nt(a, b):
    return lax.dot_general(a, b, (((1,), (1,)), ((), ())), preferred_element_type=F32)


def pack_kernel(cnt_ref, idx_ref, pts_ref, out_ref):
    sub = iota((BLK, ROWS_DEV), 0)
    lane = iota((BLK, ROWS_DEV), 1)
    want = jnp.full((BLK, ROWS_DEV), -1, jnp.int32)
    for q in range(CNT_ROW):
        want = jnp.where(sub == q, idx_ref[q], want)
    rows = jnp.dot(one_hot(lane == want), pts_ref[...], preferred_element_type=F32)
    sub = iota((BLK, D), 0)
    lane = iota((BLK, D), 1)
    for r in range(ROUNDS):
        here = jnp.logical_and(sub == CNT_ROW, lane == r)
        rows = jnp.where(here, cnt_ref[r].astype(F32), rows)
    rows = rows.astype(BF16)
    for i in range(PLANE):
        out_ref[i] = rows


def compact_kernel(recv_ref, out_ref):
    place = lax.axis_index("y") * NX + lax.axis_index("x")
    n = PLANE * BLK
    head = recv_ref[:, 0:128]
    src = iota((n, n), 0)
    dst = iota((n, n), 1)
    is_cnt = src % BLK == CNT_ROW
    own = one_hot(jnp.logical_and(is_cnt, src // BLK == dst // BLK))
    before = one_hot(jnp.logical_and(is_cnt, src // BLK < dst // BLK))
    contract = (((0,), (0,)), ((), ()))
    cnt = lax.dot_general(head, own, contract, preferred_element_type=F32)[:16]
    off = lax.dot_general(head, before, contract, preferred_element_type=F32)[:16]
    r = iota((16, n), 0)
    q = iota((16, n), 1) % BLK
    j = (q % CAP).astype(F32)
    live = jnp.logical_and(q < CNT_ROW, q // CAP == r)
    live = jnp.logical_and(live, j < cnt)
    live = jnp.logical_and(live, off + j == place.astype(F32))
    rows = jnp.dot(one_hot(live), recv_ref[...], preferred_element_type=F32)
    rows = rows[0:4].astype(BF16)
    for i in range(NZ):
        out_ref[i] = rows


def spread_kernel(recv_ref, out_ref, tmp_ref):
    for z in range(NZ):
        tmp_ref[4 * z : 4 * z + 4, :] = recv_ref[z].astype(F32)
    m = iota((KEEP, 4 * NZ), 0)
    k = iota((KEEP, 4 * NZ), 1)
    sel = one_hot(k == 4 * (m % NZ) + m // NZ)
    rows = jnp.dot(sel, tmp_ref[...].astype(BF16), preferred_element_type=F32)
    rows = rows.astype(BF16)
    for i in range(PLANE):
        out_ref[i] = rows


def round_mins(cands_ref, pts):
    cands = cands_ref[...]
    prod = dot_nt(cands, pts)
    wide = cands.astype(F32)
    norm = jnp.sum(wide * wide, axis=1, keepdims=True)
    val = (norm - 2.0 * prod).reshape(PLANE, ROUNDS, NZ, ROWS_DEV)
    least = jnp.min(jnp.min(val, axis=0), axis=1)
    return [least[r : r + 1] for r in range(ROUNDS)]


def own_kernel(pts_ref, center_ref, cands_ref, out_ref):
    pts = pts_ref[...]
    wide = pts.astype(F32)
    sq = wide * wide
    hi = sq.astype(BF16)
    lo = (sq - hi.astype(F32)).astype(BF16)
    ones = jnp.ones((16, D), BF16)
    rows_norm = (dot_nt(ones, hi) + dot_nt(ones, lo))[0:1]
    center = jnp.broadcast_to(center_ref[...], (16, D))
    cwide = center.astype(F32)
    cnorm = jnp.sum(cwide * cwide, axis=1, keepdims=True)
    first = (cnorm - 2.0 * dot_nt(center, pts))[0:1]
    mins = round_mins(cands_ref, pts)
    out_ref[0:1] = rows_norm
    out_ref[1:2] = first
    for r in range(ROUNDS):
        out_ref[2 + r : 3 + r] = mins[r]


def other_kernel(pts_ref, own_ref, cands_ref, run_ref, sums_ref):
    mins = round_mins(cands_ref, pts_ref[...])
    rows_norm = own_ref[0:1]
    running = jnp.maximum(rows_norm + own_ref[1:2], 0.0)
    lane = iota((PLANE, 128), 1)
    sums = jnp.where(lane == 0, jnp.sum(running), 0.0)
    for r in range(ROUNDS):
        least = jnp.minimum(own_ref[2 + r : 3 + r], mins[r])
        running = jnp.minimum(running, jnp.maximum(rows_norm + least, 0.0))
        sums = jnp.where(lane == r + 1, jnp.sum(running), sums)
    run_ref[...] = running
    sums_ref[...] = sums


def relay_kernel(recv_ref, out_ref):
    total = jnp.sum(recv_ref[...], axis=0, keepdims=True)
    out_ref[...] = jnp.broadcast_to(total, (NZ * NC, 128))


def final_kernel(recv_ref, run_ref, dist_ref, weight_ref, pot_ref):
    total = jnp.sum(recv_ref[...], axis=0, keepdims=True)
    lane = iota((1, 128), 1)
    last = jnp.sum(jnp.where(lane == ROUNDS, total, 0.0), axis=1, keepdims=True)
    running = run_ref[...]
    dist_ref[...] = running.reshape(ROWS_DEV)
    weight_ref[...] = (running * (ROWS / last)).reshape(ROWS_DEV)
    pot_ref[...] = total.reshape(128)[0 : ROUNDS + 1]


def vspec():
    return pl.BlockSpec(memory_space=VMEM)


def sspec():
    return pl.BlockSpec(memory_space=SMEM)


def call(kernel, ins, outs, scratch=(), name=None):
    shapes = [jax.ShapeDtypeStruct(s, d) for s, d in outs]
    single = len(shapes) == 1
    return pl.pallas_call(
        kernel,
        in_specs=ins,
        out_specs=vspec() if single else [vspec() for _ in shapes],
        out_shape=shapes[0] if single else shapes,
        scratch_shapes=list(scratch),
        name=name,
    )


def body(points, first_center, counts, cand_index):
    pack = call(pack_kernel, [sspec(), sspec(), vspec()], [((PLANE, BLK, D), BF16)], name="pack")
    blocks = pack(counts.reshape(ROUNDS), cand_index.reshape(ROUNDS * CAP), points)
    blocks = lax.all_to_all(blocks, ("y", "x"), 0, 0)
    compact = call(compact_kernel, [vspec()], [((NZ, 4, D), BF16)], name="compact")
    mine = compact(blocks.reshape(PLANE * BLK, D))
    mine = lax.all_to_all(mine, "z", 0, 0)
    spread = call(spread_kernel, [vspec()], [((PLANE, KEEP, D), BF16)], [VMEM((4 * NZ, D), F32)], name="spread")
    cands = lax.all_to_all(spread(mine), ("y", "x"), 0, 0).reshape(HALF, D)
    others = lax.ppermute(cands, "c", [(0, 1), (1, 0)])
    own = call(own_kernel, [vspec()] * 3, [((8, ROWS_DEV), F32)], name="own")
    found = own(points, first_center.reshape(1, D), cands)
    other = call(other_kernel, [vspec()] * 3, [((1, ROWS_DEV), F32), ((PLANE, 128), F32)], name="other")
    running, sums = other(points, found, others)
    sums = lax.all_to_all(sums, ("y", "x"), 0, 0)
    relay = call(relay_kernel, [vspec()], [((NZ * NC, 128), F32)], name="relay")
    sums = lax.all_to_all(relay(sums), ("z", "c"), 0, 0)
    final = call(
        final_kernel,
        [vspec()] * 2,
        [((ROWS_DEV,), F32), ((ROWS_DEV,), F32), ((ROUNDS + 1,), F32)],
        name="final",
    )
    return tuple(final(sums, running))


def solution(mesh):
    axes = ("z", "c", "y", "x")
    grid = Mesh(mesh.devices.reshape(NZ, NC, NY, NX), axes)
    placed = (P(axes, None), P(), P(None, ("z", "c"), ("y", "x")), P(None, ("z", "c"), ("y", "x"), None))
    return jax.shard_map(
        body,
        mesh=grid,
        in_specs=placed,
        out_specs=(P(axes), P(axes), P()),
        check_vma=False,
    )
```

time: 747 us -> 124 us (0.17)
  waiting for transfers between devices: 360 us -> 0.01 us
  blocking collectives: 292 us -> 96.9 us
  local copies, waits for them, and re-layouts: 57.6 us -> 2.36 us
  other arithmetic: 17.6 us -> 0.7 us
  Pallas kernels: 0 us -> 15.4 us
  between operations: 14.5 us -> 0.66 us
    all_gather x3 -> x0, waiting for transfers between devices: 360 us -> none  [body(): lax.all_gather(local_rows, ('dp', 'shard'), axis=0, tiled=True)]
    all_gather x1 -> x0, blocking collectives: 189 us -> none  [body(): lax.all_gather(counts.reshape(rounds, 1), ('dp', 'shard'), axis=1, tiled=...]
    psum x1 -> x0, blocking collectives: 103 us -> none  [global_sum(): return lax.psum(value, ('dp', 'shard'))]
    all_to_all x0 -> x5, blocking collectives: none -> 96.9 us  [the longest x1 28.4 us: body(): mine = lax.all_to_all(mine, 'z', 0, 0)]
    slice x1 -> x0, local copies, waits for them, and re-layouts: 28.8 us -> none  [body(): slot_limit = jnp.repeat(every_count[step], cap)]
    unnamed x16 -> x6, local copies, waits for them, and re-layouts: 23.1 us -> 1.18 us
    pallas_call x0 -> x7, Pallas kernels: none -> 15.4 us  [the longest x1 3.27 us: body(): found = own(points, first_center.reshape(1, D), cands)]
    reduce_sum x7 -> x0, other arithmetic: 10.7 us -> none  [the longest x4 8.62 us: pair_dist(): cand_norm = jnp.sum(jnp.square(cands.astype(jnp.float32)), axis=1)]
  transfers between devices with their start and end apart: 3 -> 1, of which waited for: 2 -> 0; matrix products, arithmetic and copies ran while one was open for 7% -> 0% of each run, Pallas kernels for 0% -> 3%
where the time goes in v1:
time: 124 us; the launch traced here: 123 us
  blocking collectives  96.9 us (78%)
  Pallas kernels  15.4 us (12%)
  starting transfers between devices  6.78 us (5%)
  local copies, waits for them, and re-layouts  2.36 us (2%)
    all_to_all x1, blocking collectives, body(): mine = lax.all_to_all(mine, 'z', 0, 0)  28.4 us
    all_to_all x1, blocking collectives, body(): cands = lax.all_to_all(spread(mine), ('y', 'x'), 0, 0).reshape(HALF, D)  22.7 us
    all_to_all x1, blocking collectives, body(): sums = lax.all_to_all(relay(sums), ('z', 'c'), 0, 0)  18.9 us
    all_to_all x1, blocking collectives, body(): blocks = lax.all_to_all(blocks, ('y', 'x'), 0, 0)  16.7 us
    all_to_all x1, blocking collectives, body(): sums = lax.all_to_all(sums, ('y', 'x'), 0, 0)  10.2 us
    ppermute x1, starting transfers between devices, body(): others = lax.ppermute(cands, 'c', [(0, 1), (1, 0)])  6.78 us
    pallas_call x1, Pallas kernels, body(): found = own(points, first_center.reshape(1, D), cands)  3.27 us
    pallas_call x1, Pallas kernels, body(): running, sums = other(points, found, others)  2.98 us
  transfers between devices with their start and end apart: 1, of which 0 were waited for; matrix products, arithmetic and copies ran while one was open for 0% of the time, Pallas kernels for 3%

profile of v1, /device:TPU:1, one launch (start us, length us, event | category | flops | bytes accessed | tf_op | source)
XLA Modules:
  0.0 122.8 jit_solution(18429997712064441885)
XLA Ops:
  0.6 0.7 reduce
  1.3 0.6 reshape.27.idx_ref
  1.9 2.1 %pack.1 = bf16[16,16,1024]{2,1,0:T(8,128)(2,1)} custom-call(s32[3]{0:T(128)} %bitcast.18, s32[12]{0:T(128)} %reshape.27.idx_ref, bf16[256,1024]{1,0:T(8,128)(2,1)} %pts_ref.5), custom_call_target="tpu_custom_call" | custom-call | tf_op jit(solution)/shard_map/pack/pallas_call | solution.py:173
  4.0 16.7 %all_to_all.37 = bf16[16,16,1024]{2,1,0:T(8,128)(2,1)} all-to-all(bf16[16,16,1024]{2,1,0:T(8,128)(2,1)} %pack.1), channel_id=1, replica_groups=mesh['z'=16,'c'=2,'y'=4,'x'=4] {'y','x'}, dimensions={0} | all-to-all | bytes 1048576 | tf_op jit(solution)/shard_map/all_to_all | solution.py:174
  20.6 2.0 %compact.1 = bf16[16,4,1024]{2,1,0:T(4,128)(2,1)} custom-call(bf16[256,1024]{1,0:T(8,128)(2,1)} %bitcast.13), custom_call_target="tpu_custom_call" | custom-call | tf_op jit(solution)/shard_map/compact/pallas_call | solution.py:176
  22.7 28.4 %all_to_all.38.recv_ref = bf16[16,4,1024]{2,1,0:T(4,128)(2,1)} all-to-all(bf16[16,4,1024]{2,1,0:T(4,128)(2,1)} %compact.1), channel_id=1, replica_groups=mesh['z'=16,'c'=2,'y'=4,'x'=4] {'z'}, dimensions={0} | all-to-all | bytes 262144 | tf_op jit(solution)/shard_map/all_to_all | solution.py:177
  51.1 2.4 %spread.1 = bf16[16,48,1024]{2,1,0:T(8,128)(2,1)} custom-call(bf16[16,4,1024]{2,1,0:T(4,128)(2,1)} %all_to_all.38.recv_ref), custom_call_target="tpu_custom_call" | custom-call | tf_op jit(solution)/shard_map/spread/pallas_call | solution.py:179
  53.5 0.0 copy-start.2
  53.5 22.7 %all_to_all.39 = bf16[16,48,1024]{2,1,0:T(8,128)(2,1)S(1)} all-to-all(bf16[16,48,1024]{2,1,0:T(8,128)(2,1)} %spread.1), channel_id=1, replica_groups=mesh['z'=16,'c'=2,'y'=4,'x'=4] {'y','x'}, dimensions={0} | all-to-all | bytes 3145728 | tf_op jit(solution)/shard_map/all_to_all | solution.py:179
  76.2 0.0 copy-start
  76.2 6.8 %collective-permute-start = (bf16[768,1024]{1,0:T(8,128)(2,1)S(1)}, bf16[768,1024]{1,0:T(8,128)(2,1)S(1)}, u32[]{:S(2)}, u32[]{:S(2)}) collective-permute-start(bf16[768,1024]{1,0:T(8,128)(2,1)S(1)} %bitcast.11), channel_id=1, source_target_pairs={{0,16},{16,0},{1,17},{17,1},{2,18},{18,2},{3,19},{19,3},{4,20},{20... | collective-permute-start | bytes 4718600 | tf_op jit(solution)/shard_map/ppermute | solution.py:180
  83.0 0.0 copy-done.2
  83.0 0.6 reshape.25.center_ref
  83.6 0.0 copy-done
  83.6 3.3 %own.1.own_ref = f32[8,256]{1,0:T(8,128)} custom-call(bf16[256,1024]{1,0:T(8,128)(2,1)} %pts_ref.5, bf16[1,1024]{1,0:T(2,128)(2,1)} %reshape.25.center_ref, bf16[768,1024]{1,0:T(8,128)(2,1)} %bitcast.12), custom_call_target="tpu_custom_call" | custom-call | tf_op jit(solution)/shard_map/own/pallas_call | solution.py:182
  86.8 0.0 collective-permute-done.cands_ref
  86.8 0.0 copy-start.1
  86.8 1.2 copy-done.1
  88.0 3.0 %other.1 = (f32[1,256]{1,0:T(1,128)}, f32[16,128]{1,0:T(8,128)}) custom-call(bf16[256,1024]{1,0:T(8,128)(2,1)} %pts_ref.5, f32[8,256]{1,0:T(8,128)} %own.1.own_ref, bf16[768,1024]{1,0:T(8,128)(2,1)} %copy-done.1), custom_call_target="tpu_custom_call" | custom-call | tf_op jit(solution)/shard_map/other/pallas_call | solution.py:184
  91.0 10.2 %all_to_all.40 = f32[16,1,128]{2,1,0:T(1,128)} all-to-all(f32[16,1,128]{2,1,0:T(1,128)} %bitcast.17), channel_id=1, replica_groups=mesh['z'=16,'c'=2,'y'=4,'x'=4] {'y','x'}, dimensions={0} | all-to-all | bytes 16384 | tf_op jit(solution)/shard_map/all_to_all | solution.py:185
  101.2 1.3 %relay.1 = f32[32,128]{1,0:T(8,128)} custom-call(f32[16,128]{1,0:T(8,128)} %bitcast.16), custom_call_target="tpu_custom_call" | custom-call | tf_op jit(solution)/shard_map/relay/pallas_call | solution.py:187
  102.5 18.9 %all_to_all.41 = f32[32,1,128]{2,1,0:T(1,128)} all-to-all(f32[32,1,128]{2,1,0:T(1,128)} %bitcast.15), channel_id=1, replica_groups=mesh['z'=16,'c'=2,'y'=4,'x'=4] {'z','c'}, dimensions={0} | all-to-all | bytes 32768 | tf_op jit(solution)/shard_map/all_to_all | solution.py:187
  121.4 1.4 %final.1 = (f32[256]{0:T(256)}, f32[256]{0:T(256)}, f32[4]{0:T(128)}) custom-call(f32[32,128]{1,0:T(8,128)} %bitcast.14, f32[1,256]{1,0:T(1,128)} %get-tuple-element.6.run_ref), custom_call_target="tpu_custom_call" | custom-call | tf_op jit(solution)/shard_map/final/pallas_call | solution.py:194
Async XLA Ops:
  53.5 29.5 %copy-start.2 = (bf16[1024]{0:T(1024)(128)(2,1)S(1)}, bf16[1024]{0:T(1024)(128)(2,1)}, u32[]{:S(2)}) copy-start(bf16[1024]{0:T(1024)(128)(2,1)} %param.5) | copy-start | bytes 6148
  76.2 7.4 %copy-start = (bf16[16,48,1024]{2,1,0:T(8,128)(2,1)}, bf16[16,48,1024]{2,1,0:T(8,128)(2,1)S(1)}, u32[]{:S(2)}) copy-start(bf16[16,48,1024]{2,1,0:T(8,128)(2,1)S(1)} %all_to_all.39) | copy-start | bytes 4718596
  76.2 10.7 %collective-permute-start = (bf16[768,1024]{1,0:T(8,128)(2,1)S(1)}, bf16[768,1024]{1,0:T(8,128)(2,1)S(1)}, u32[]{:S(2)}, u32[]{:S(2)}) collective-permute-start(bf16[768,1024]{1,0:T(8,128)(2,1)S(1)} %bitcast.11), channel_id=1, source_target_pairs={{0,16},{16,0},{1,17},{17,1},{2,18},{18,2},{3,19},{19,3},{4,20},{20... | collective-permute-start | bytes 4718600 | tf_op jit(solution)/shard_map/ppermute | solution.py:180
  86.8 1.2 copy-start.1

commit v2 on v1

--- a/solution.py
+++ b/solution.py
@@ -36,12 +36,21 @@
     return lax.dot_general(a, b, (((1,), (1,)), ((), ())), preferred_element_type=F32)
 
 
-def pack_kernel(cnt_ref, idx_ref, pts_ref, out_ref):
+def pack_kernel(cnt_hbm, idx_hbm, pts_hbm, out_ref, cnt_ref, idx_ref, pts_ref, sem):
+    fetch_idx = pltpu.make_async_copy(idx_hbm, idx_ref, sem.at[0])
+    fetch_cnt = pltpu.make_async_copy(cnt_hbm, cnt_ref, sem.at[1])
+    fetch = pltpu.make_async_copy(pts_hbm, pts_ref, sem.at[2])
+    fetch_idx.start()
+    fetch_cnt.start()
+    fetch.start()
+    fetch_idx.wait()
+    fetch_cnt.wait()
     sub = iota((BLK, ROWS_DEV), 0)
     lane = iota((BLK, ROWS_DEV), 1)
     want = jnp.full((BLK, ROWS_DEV), -1, jnp.int32)
     for q in range(CNT_ROW):
-        want = jnp.where(sub == q, idx_ref[q], want)
+        want = jnp.where(sub == q, idx_ref[q // CAP, 0, 0, q % CAP], want)
+    fetch.wait()
     rows = jnp.dot(one_hot(lane == want), pts_ref[...], preferred_element_type=F32)
     sub = iota((BLK, D), 0)
     lane = iota((BLK, D), 1)
@@ -107,7 +116,7 @@
     lo = (sq - hi.astype(F32)).astype(BF16)
     ones = jnp.ones((16, D), BF16)
     rows_norm = (dot_nt(ones, hi) + dot_nt(ones, lo))[0:1]
-    center = jnp.broadcast_to(center_ref[...], (16, D))
+    center = jnp.broadcast_to(center_ref[...].reshape(1, D), (16, D))
     cwide = center.astype(F32)
     cnorm = jnp.sum(cwide * cwide, axis=1, keepdims=True)
     first = (cnorm - 2.0 * dot_nt(center, pts))[0:1]
@@ -151,26 +160,43 @@
     return pl.BlockSpec(memory_space=VMEM)
 
 
-def sspec():
-    return pl.BlockSpec(memory_space=SMEM)
-
-
-def call(kernel, ins, outs, scratch=(), name=None):
-    shapes = [jax.ShapeDtypeStruct(s, d) for s, d in outs]
+def call(kernel, ins, outs, scratch=(), name=None, near=True):
+    shapes = [VMEM(s, d) if near else jax.ShapeDtypeStruct(s, d) for s, d in outs]
     single = len(shapes) == 1
-    return pl.pallas_call(
+    kern = pl.pallas_call(
         kernel,
         in_specs=ins,
         out_specs=vspec() if single else [vspec() for _ in shapes],
         out_shape=shapes[0] if single else shapes,
         scratch_shapes=list(scratch),
+        compiler_params=pltpu.CompilerParams(vmem_limit_bytes=16 << 20),
         name=name,
     )
 
+    def run(*args):
+        placed = []
+        for a, i in zip(args, ins):
+            space = VMEM if i.memory_space == VMEM else pltpu.HBM
+            placed.append(pltpu.with_memory_space_constraint(a, space))
+        return kern(*placed)
+
+    return run
+
 
 def body(points, first_center, counts, cand_index):
-    pack = call(pack_kernel, [sspec(), sspec(), vspec()], [((PLANE, BLK, D), BF16)], name="pack")
-    blocks = pack(counts.reshape(ROUNDS), cand_index.reshape(ROUNDS * CAP), points)
+    pack = call(
+        pack_kernel,
+        [pl.BlockSpec(memory_space=pl.ANY)] * 3,
+        [((PLANE, BLK, D), BF16)],
+        [
+            SMEM((ROUNDS,), jnp.int32),
+            SMEM((ROUNDS, 1, 1, CAP), jnp.int32),
+            VMEM((ROWS_DEV, D), BF16),
+            pltpu.SemaphoreType.DMA((3,)),
+        ],
+        name="pack",
+    )
+    blocks = pack(counts.reshape(ROUNDS), cand_index, points)
     blocks = lax.all_to_all(blocks, ("y", "x"), 0, 0)
     compact = call(compact_kernel, [vspec()], [((NZ, 4, D), BF16)], name="compact")
     mine = compact(blocks.reshape(PLANE * BLK, D))
@@ -179,7 +205,7 @@
     cands = lax.all_to_all(spread(mine), ("y", "x"), 0, 0).reshape(HALF, D)
     others = lax.ppermute(cands, "c", [(0, 1), (1, 0)])
     own = call(own_kernel, [vspec()] * 3, [((8, ROWS_DEV), F32)], name="own")
-    found = own(points, first_center.reshape(1, D), cands)
+    found = own(points, first_center, cands)
     other = call(other_kernel, [vspec()] * 3, [((1, ROWS_DEV), F32), ((PLANE, 128), F32)], name="other")
     running, sums = other(points, found, others)
     sums = lax.all_to_all(sums, ("y", "x"), 0, 0)
@@ -190,6 +216,7 @@
         [vspec()] * 2,
         [((ROWS_DEV,), F32), ((ROWS_DEV,), F32), ((ROUNDS + 1,), F32)],
         name="final",
+        near=False,
     )
     return tuple(final(sums, running))
 

time: 124 us -> 109 us (0.88)
  Pallas kernels: 15.4 us -> 4.53 us
  local copies, waits for them, and re-layouts: 2.36 us -> 0.01 us
  waiting for transfers between devices: 0.01 us -> 1.87 us
  blocking collectives: 96.9 us -> 95.2 us
    pallas_call x7, Pallas kernels: 15.4 us -> 4.53 us  [run(): return kern(*placed)]
    ppermute x1, waiting for transfers between devices: 0.01 us -> 1.87 us  [body(): others = lax.ppermute(cands, 'c', [(0, 1), (1, 0)])]
  transfers between devices with their start and end apart: 1 -> 1, of which waited for: 0 -> 1; matrix products, arithmetic and copies ran while one was open for 0% -> 0% of each run, Pallas kernels for 3% -> 1%
where the time goes in v2:
time: 109 us
  blocking collectives  95.2 us (87%)
  starting transfers between devices  6.68 us (6%)
  Pallas kernels  4.53 us (4%)
  waiting for transfers between devices  1.87 us (2%)
    all_to_all x1, blocking collectives, body(): mine = lax.all_to_all(mine, 'z', 0, 0)  27.5 us
    all_to_all x1, blocking collectives, body(): cands = lax.all_to_all(spread(mine), ('y', 'x'), 0, 0).reshape(HALF, D)  22.5 us
    all_to_all x1, blocking collectives, body(): sums = lax.all_to_all(relay(sums), ('z', 'c'), 0, 0)  19.2 us
    all_to_all x1, blocking collectives, body(): blocks = lax.all_to_all(blocks, ('y', 'x'), 0, 0)  17 us
    all_to_all x1, blocking collectives, body(): sums = lax.all_to_all(sums, ('y', 'x'), 0, 0)  9 us
    ppermute x1, starting transfers between devices, body(): others = lax.ppermute(cands, 'c', [(0, 1), (1, 0)])  6.68 us
    pallas_call x7, Pallas kernels, run(): return kern(*placed)  4.53 us
  transfers between devices with their start and end apart: 1, of which 1 were waited for; matrix products, arithmetic and copies ran while one was open for 0% of the time, Pallas kernels for 1%

profile of v2, /device:TPU:1, one launch (start us, length us, event | category | flops | bytes accessed | tf_op | source)
XLA Modules:
  0.0 109.0 jit_solution(207193606920943643)
XLA Ops:
  0.6 1.3 %pack.1 = bf16[16,16,1024]{2,1,0:T(8,128)(2,1)S(1)} custom-call(s32[3]{0:T(128)} %bitcast.18, s32[3,1,1,4]{3,2,1,0:T(1,128)} %idx_hbm.1, bf16[256,1024]{1,0:T(8,128)(2,1)} %pts_ref.3), custom_call_target="tpu_custom_call" | custom-call | tf_op jit(solution)/shard_map/pack/pallas_call | solution.py:181
  1.9 17.0 %all_to_all.37 = bf16[16,16,1024]{2,1,0:T(8,128)(2,1)S(1)} all-to-all(bf16[16,16,1024]{2,1,0:T(8,128)(2,1)S(1)} %pack.1), channel_id=1, replica_groups=mesh['z'=16,'c'=2,'y'=4,'x'=4] {'y','x'}, dimensions={0} | all-to-all | bytes 1048576 | tf_op jit(solution)/shard_map/all_to_all | solution.py:200
  18.9 0.3 compact.1
  19.3 27.5 %all_to_all.38.recv_ref = bf16[16,4,1024]{2,1,0:T(4,128)(2,1)S(1)} all-to-all(bf16[16,4,1024]{2,1,0:T(4,128)(2,1)S(1)} %compact.1), channel_id=1, replica_groups=mesh['z'=16,'c'=2,'y'=4,'x'=4] {'z'}, dimensions={0} | all-to-all | bytes 262144 | tf_op jit(solution)/shard_map/all_to_all | solution.py:203
  46.7 0.3 spread.1
  47.0 0.0 copy-start
  47.1 0.0 copy-start.1
  47.1 22.5 %all_to_all.39 = bf16[16,48,1024]{2,1,0:T(8,128)(2,1)S(1)} all-to-all(bf16[16,48,1024]{2,1,0:T(8,128)(2,1)S(1)} %spread.1), channel_id=1, replica_groups=mesh['z'=16,'c'=2,'y'=4,'x'=4] {'y','x'}, dimensions={0} | all-to-all | bytes 3145728 | tf_op jit(solution)/shard_map/all_to_all | solution.py:205
  69.5 6.7 %collective-permute-start = (bf16[768,1024]{1,0:T(8,128)(2,1)S(1)}, bf16[768,1024]{1,0:T(8,128)(2,1)S(1)}, u32[]{:S(2)}, u32[]{:S(2)}) collective-permute-start(bf16[768,1024]{1,0:T(8,128)(2,1)S(1)} %bitcast.11), channel_id=1, source_target_pairs={{0,16},{16,0},{1,17},{17,1},{2,18},{18,2},{3,19},{19,3},{4,20},{20... | collective-permute-start | bytes 4718600 | tf_op jit(solution)/shard_map/ppermute | solution.py:206
  76.2 0.0 copy-done
  76.2 0.0 copy-done.1
  76.2 1.1 %own.1.own_ref = f32[8,256]{1,0:T(8,128)S(1)} custom-call(bf16[256,1024]{1,0:T(8,128)(2,1)S(1)} %copy-done, bf16[1024]{0:T(1024)(128)(2,1)S(1)} %copy-done.1, bf16[768,1024]{1,0:T(8,128)(2,1)S(1)} %bitcast.12), custom_call_target="tpu_custom_call" | custom-call | tf_op jit(solution)/shard_map/own/pallas_call | solution.py:181
  77.4 1.9 %collective-permute-done.cands_ref = bf16[768,1024]{1,0:T(8,128)(2,1)S(1)} collective-permute-done((bf16[768,1024]{1,0:T(8,128)(2,1)S(1)}, bf16[768,1024]{1,0:T(8,128)(2,1)S(1)}, u32[]{:S(2)}, u32[]{:S(2)}) %collective-permute-start) | collective-permute-done | bytes 1572896 | tf_op jit(solution)/shard_map/ppermute | solution.py:206
  79.2 0.8 other.1
  80.1 9.0 %all_to_all.40 = f32[16,1,128]{2,1,0:T(1,128)S(1)} all-to-all(f32[16,1,128]{2,1,0:T(1,128)S(1)} %bitcast.17), channel_id=1, replica_groups=mesh['z'=16,'c'=2,'y'=4,'x'=4] {'y','x'}, dimensions={0} | all-to-all | bytes 16384 | tf_op jit(solution)/shard_map/all_to_all | solution.py:211
  89.1 19.2 %all_to_all.41 = f32[32,1,128]{2,1,0:T(1,128)S(1)} all-to-all(f32[32,1,128]{2,1,0:T(1,128)S(1)} %bitcast.15), channel_id=1, replica_groups=mesh['z'=16,'c'=2,'y'=4,'x'=4] {'z','c'}, dimensions={0} | all-to-all | bytes 32768 | tf_op jit(solution)/shard_map/all_to_all | solution.py:213
  108.3 0.7 final.1
  (1 shorter events, 0.0 us)
Async XLA Ops:
  47.0 29.2 %copy-start = (bf16[256,1024]{1,0:T(8,128)(2,1)S(1)}, bf16[256,1024]{1,0:T(8,128)(2,1)}, u32[]{:S(2)}) copy-start(bf16[256,1024]{1,0:T(8,128)(2,1)} %pts_ref.3) | copy-start | bytes 1572868
  47.1 29.2 %copy-start.1 = (bf16[1024]{0:T(1024)(128)(2,1)S(1)}, bf16[1024]{0:T(1024)(128)(2,1)}, u32[]{:S(2)}) copy-start(bf16[1024]{0:T(1024)(128)(2,1)} %center_ref.1) | copy-start | bytes 6148
  69.5 9.7 %collective-permute-start = (bf16[768,1024]{1,0:T(8,128)(2,1)S(1)}, bf16[768,1024]{1,0:T(8,128)(2,1)S(1)}, u32[]{:S(2)}, u32[]{:S(2)}) collective-permute-start(bf16[768,1024]{1,0:T(8,128)(2,1)S(1)} %bitcast.11), channel_id=1, source_target_pairs={{0,16},{16,0},{1,17},{17,1},{2,18},{18,2},{3,19},{19,3},{4,20},{20... | collective-permute-start | bytes 4718600 | tf_op jit(solution)/shard_map/ppermute | solution.py:206
